TPU v7x, 32 devices: a whole 2x2x4 slice. The times are simulated.
32 devices in a mesh: grp: 8 (over y, x, core), top: 4 (over z).
Axes of the slice: x: 2, y: 2, z: 4, core: 2. Of those that a mesh axis runs over, the one named last changes fastest.
Arguments:
- basis_grad: float32 [8, 4, 512, 384], P('grp', 'top'), may hold values from -6 to 6
- leaf_q: float32 [8, 4, 512, 384], P('grp', 'top'), may hold values from -0.25 to 0.25
- leaf_rinv: float32 [8, 4, 384, 384], P('grp', 'top'), may hold values from -5 to 4, as said below
- merge_q1: float32 [8, 4, 384, 384], P('grp', 'top'), may hold values from -0.3125 to 0.3125
- merge_q2: float32 [4, 384, 384], P('top', 'grp'), may hold values from -0.15625 to 0.15625
Outputs:
- data_grad: float32 [8, 4, 512, 384], P('grp', 'top')
Inputs may be any that keep to these rules, and one draw needn't show every extreme that they name: Each leaf_rinv[i,g] is upper triangular with a diagonal between 1 and 4.
All inputs are finite; a program needn't handle non-finite values.
Results may differ from a plain program's by a relative error of at most 0.00023.
Values sent between devices are 32-bit elements; how exact they have to be, the bound alone decides.
A program may use at most 64 MiB of HBM per device.

v0:
```python
import jax
import jax.numpy as jnp
from jax import lax
from jax.sharding import PartitionSpec as P


def product(former, latter, former_dim, latter_dim):
    return lax.dot_general(
        former,
        latter,
        (((former_dim,), (latter_dim,)), ((), ())),
        precision=lax.Precision.HIGH,
        preferred_element_type=jnp.float32,
    )


def symmetrize(matrix):
    return jnp.tril(matrix) + jnp.tril(matrix, -1).T


def per_device(basis_grad, leaf_q, leaf_rinv, merge_q1, merge_q2):
    cotangent = basis_grad[0, 0]
    leaf_basis = leaf_q[0, 0]
    inverse = leaf_rinv[0, 0]
    first_block = merge_q1[0, 0]
    second_factor = lax.all_gather(merge_q2[0], "grp", axis=0, tiled=True)
    projected = product(leaf_basis, cotangent, 0, 0)
    combined = product(first_block, second_factor, 1, 0)
    top_adjoint = -lax.psum(product(projected, combined, 0, 0), ("grp", "top"))
    top_sym = symmetrize(top_adjoint)
    spread = product(leaf_basis, combined, 1, 0)
    outer = product(inverse, combined, 1, 0)
    inner = cotangent + product(spread, top_sym, 1, 0)
    result = product(inner, outer, 1, 1)
    return result[None, None]


def solution(mesh):
    placed = (
        P("grp", "top", None, None),
        P("grp", "top", None, None),
        P("grp", "top", None, None),
        P("grp", "top", None, None),
        P("top", "grp", None),
    )
    return jax.shard_map(
        per_device,
        mesh=mesh,
        in_specs=placed,
        out_specs=P("grp", "top", None, None),
        check_vma=False,
    )
```

profile of v0, /device:TPU:0, one launch (start us, length us, event | category | flops | bytes accessed | tf_op | source)
XLA Modules:
  0.0 163.3 jit_solution(13517483141683757118)
XLA Ops:
  6.5 0.0 copy-start
  6.5 0.0 copy-start.2
  6.5 0.0 all-reduce.2.cloned.1.call-start
  6.5 11.9 %all-gather = f32[1,384,384]{2,1,0:T(8,128)S(1)} all-gather(f32[1,48,384]{2,1,0:T(8,128)} %param.9), channel_id=2, replica_groups=mesh['grp'=8,'top'=4] {'grp'}, dimensions={1}, use_global_device_ids=true | all-gather | bytes 663552 | tf_op jit(solution)/shard_map/all_gather | solution.py:26
  18.4 0.0 copy-done.2
  18.4 0.0 copy-start.1
  18.4 0.7 fusion.7
  19.2 0.0 copy-done
  19.2 0.4 copy-done.1
  19.6 0.8 fusion
  20.4 1.6 fusion.17
  22.0 0.0 copy-start.3
  22.0 0.0 all-reduce.2.cloned.1.call-update
  22.0 1.0 copy-done.3
  23.0 1.1 fusion.5
  24.2 1.2 fusion.2
  25.3 124.4 %all-reduce.2.cloned.1.call-done = f32[384,384]{1,0:T(8,128)} async-done(((f32[384,384]{1,0:T(8,128)}), f32[384,384]{1,0:T(8,128)}) %all-reduce.2.cloned.1.call-update) | async-done | bytes 589840 | tf_op jit(solution)/shard_map/psum | solution.py:29
  149.8 1.1 neg.3
  150.9 1.1 copy.6
  151.9 2.7 %convolution_add_fusion = f32[512,384]{1,0:T(8,128)S(1)} fusion(f32[384,512]{1,0:T(8,128)S(1)} %fusion.2, f32[1,1,512,384]{3,2,1,0:T(8,128)S(1)} %copy-done.1, f32[384,384]{0,1:T(8,128)} %copy.6, s32[384]{0:T(512)S(1)} %iota_add_fusion, f32[384,384]{1,0:T(8,128)} %all-reduce.2.cloned.1.call-done), kind=kOutput, calls=%fused_computation.1 | convolution fusion | flops 454066176 | bytes 3540480 | tf_op jit(solution)/shard_map/dot_general | solution.py:8
  154.7 1.8 %convolution_bitcast_fusion = f32[1,1,512,384]{3,2,1,0:T(8,128)} fusion(f32[512,384]{1,0:T(8,128)S(1)} %convolution_add_fusion, f32[384,384]{1,0:T(8,128)S(1)} %fusion.5), kind=kOutput, calls=%fused_computation | convolution fusion | flops 452984832 | bytes 2162688 | tf_op jit(solution)/shard_map/dot_general | solution.py:8
  (1 shorter events, 0.0 us)
Async XLA Ops:
  6.5 12.6 %copy-start = (f32[1,1,512,384]{3,2,1,0:T(8,128)S(1)}, f32[1,1,512,384]{3,2,1,0:T(8,128)}, u32[]{:S(2)}) copy-start(f32[1,1,512,384]{3,2,1,0:T(8,128)} %param.6) | copy-start | bytes 2359300
  6.5 11.9 %copy-start.2 = (f32[1,1,384,384]{3,2,1,0:T(8,128)S(1)}, f32[1,1,384,384]{3,2,1,0:T(8,128)}, u32[]{:S(2)}) copy-start(f32[1,1,384,384]{3,2,1,0:T(8,128)} %param.8) | copy-start | bytes 1769476
  6.5 143.2 %all-reduce.2.cloned.1.call-start = ((), (), s32[]{:S(2)}) async-start(), calls=%async_computation | async-start | bytes 1179648 | tf_op jit(solution)/shard_map/psum | solution.py:29
  18.4 1.1 copy-start.1
  22.0 1.1 copy-start.3
Sparse Core Ops, SparseCore 0:
  22.1 127.6 all-reduce.1
where the time goes:
time: 164 us; the launch traced here: 163 us
  waiting for transfers between devices  124 us (76%)
  between operations  13.4 us (8%)
  blocking collectives  11.9 us (7%)
  matrix products  9.86 us (6%)
  local copies, waits for them, and re-layouts  2.51 us (2%)
    psum x1, waiting for transfers between devices, per_device(): top_adjoint = -lax.psum(product(projected, combined, 0, 0), ('grp', 'top'))  124 us
    all_gather x1, blocking collectives, per_device(): second_factor = lax.all_gather(merge_q2[0], 'grp', axis=0, tiled=True)  11.9 us
    dot_general x7, matrix products, product(): lax.dot_general(former, latter, (((former_dim,), (latter_dim,)), ((), ())...  9.86 us
  transfers between devices with their start and end apart: 1, of which 1 were waited for; matrix products, arithmetic and copies ran while one was open for 1% of the time, Pallas kernels for 0%

commit v1 on v0

--- a/solution.py
+++ b/solution.py
@@ -26,7 +26,9 @@
     second_factor = lax.all_gather(merge_q2[0], "grp", axis=0, tiled=True)
     projected = product(leaf_basis, cotangent, 0, 0)
     combined = product(first_block, second_factor, 1, 0)
-    top_adjoint = -lax.psum(product(projected, combined, 0, 0), ("grp", "top"))
+    top_adjoint = -jnp.sum(
+        lax.all_gather(product(projected, combined, 0, 0), ("grp", "top")), axis=0
+    )
     top_sym = symmetrize(top_adjoint)
     spread = product(leaf_basis, combined, 1, 0)
     outer = product(inverse, combined, 1, 0)

time: 164 us -> 171 us (1.043)
  other arithmetic: 1.11 us -> 8.12 us
  matrix products: 9.86 us -> 13 us
  waiting for transfers between devices: 124 us -> 122 us
    psum x1 -> x0, waiting for transfers between devices: 124 us -> none  [per_device(): top_adjoint = -lax.psum(product(projected, combined, 0, 0), ('grp', 'top'))]
    all_gather x0 -> x1, waiting for transfers between devices: none -> 122 us  [per_device(): lax.all_gather(product(projected, combined, 0, 0), ('grp', 'top'))]
    reduce_sum x0 -> x1, other arithmetic: none -> 7.26 us  [per_device(): jnp.sum(lax.all_gather(product(projected, combined, 0, 0), ('grp', 'top')...]
    dot_general x7, matrix products: 9.86 us -> 13 us  [product(): lax.dot_general(former, latter, (((former_dim,), (latter_dim,)), ((), ())...]
  transfers between devices with their start and end apart: 1 -> 1, of which waited for: 1 -> 1; matrix products, arithmetic and copies ran while one was open for 1% -> 2% of each run, Pallas kernels for 0% -> 0%
where the time goes in v1:
time: 171 us; the launch traced here: 170 us
  waiting for transfers between devices  122 us (71%)
  between operations  13.4 us (8%)
  matrix products  13 us (8%)
  blocking collectives  11.9 us (7%)
  other arithmetic  8.12 us (5%)
  local copies, waits for them, and re-layouts  2.12 us (1%)
    all_gather x1, waiting for transfers between devices, per_device(): lax.all_gather(product(projected, combined, 0, 0), ('grp', 'top'))  122 us
    dot_general x7, matrix products, product(): lax.dot_general(former, latter, (((former_dim,), (latter_dim,)), ((), ())...  13 us
    all_gather x1, blocking collectives, per_device(): second_factor = lax.all_gather(merge_q2[0], 'grp', axis=0, tiled=True)  11.9 us
    reduce_sum x1, other arithmetic, per_device(): jnp.sum(lax.all_gather(product(projected, combined, 0, 0), ('grp', 'top')...  7.26 us
  transfers between devices with their start and end apart: 1, of which 1 were waited for; matrix products, arithmetic and copies ran while one was open for 2% of the time, Pallas kernels for 0%

profile of v1, /device:TPU:0, one launch (start us, length us, event | category | flops | bytes accessed | tf_op | source)
XLA Modules:
  0.0 170.3 jit_solution(14252127622664350674)
XLA Ops:
  6.5 0.0 copy-start
  6.5 0.0 copy-start.1
  6.5 0.0 all-gather.4.cloned.1.call-start
  6.5 11.9 %all-gather = f32[1,384,384]{2,1,0:T(8,128)S(1)} all-gather(f32[1,48,384]{2,1,0:T(8,128)} %param.9), channel_id=2, replica_groups=mesh['grp'=8,'top'=4] {'grp'}, dimensions={1}, use_global_device_ids=true | all-gather | bytes 663552 | tf_op jit(solution)/shard_map/all_gather | solution.py:26
  18.4 1.8 %fusion.9 = f32[384,384]{1,0:T(8,128)S(1)} fusion(f32[1,384,384]{2,1,0:T(8,128)S(1)} %all-gather, f32[1,1,384,384]{3,2,1,0:T(8,128)} %param.8), kind=kOutput, calls=%fused_computation.11 | convolution fusion | flops 339738624 | bytes 1769472 | tf_op jit(solution)/shard_map/dot_general | solution.py:8
  20.2 0.0 copy-done
  20.2 1.9 %fusion = f32[384,384]{1,0:T(8,128)S(1)} fusion(f32[1,1,512,384]{3,2,1,0:T(8,128)S(1)} %copy-done, f32[1,1,512,384]{3,2,1,0:T(8,128)} %param.5), kind=kOutput, calls=%fused_computation.2 | convolution fusion | flops 452984832 | bytes 2162688 | tf_op jit(solution)/shard_map/dot_general | solution.py:8
  22.2 1.6 fusion.17
  23.8 0.0 all-gather.4.cloned.1.call-update
  23.8 2.2 %fusion.5 = f32[384,384]{1,0:T(8,128)S(1)} fusion(f32[384,384]{1,0:T(8,128)S(1)} %fusion.9, f32[1,1,384,384]{3,2,1,0:T(8,128)} %param.7), kind=kOutput, calls=%fused_computation.7 | convolution fusion | flops 339738624 | bytes 1769472 | tf_op jit(solution)/shard_map/dot_general | solution.py:8
  26.0 1.2 fusion.2
  27.1 121.8 %all-gather.4.cloned.1.call-done = f32[12288,384]{1,0:T(8,128)} async-done(((f32[384,384]{1,0:T(8,128)}), f32[12288,384]{1,0:T(8,128)}) %all-gather.4.cloned.1.call-update) | async-done | bytes 18874384 | tf_op jit(solution)/shard_map/all_gather | solution.py:30
  148.9 7.3 %reduce_sum.9 = f32[384,384]{1,0:T(8,128)S(1)} reduce(f32[32,384,384]{2,1,0:T(8,128)} %bitcast.33, f32[]{:T(128)} %constant.4.clone.1), dimensions={0}, to_apply=%region_0.0 | reduce | flops 4571136 | bytes 19464196 | tf_op jit(solution)/shard_map/reduce_sum | solution.py:29
  156.2 0.9 neg.7
  157.0 2.1 %copy.7 = f32[384,384]{0,1:T(8,128)} copy(f32[384,384]{1,0:T(8,128)} %neg.7) | data formatting | bytes 1179648 | tf_op jit(solution)/shard_map/neg | solution.py:29
  159.1 0.0 copy-done.1
  159.1 2.6 %convolution_add_fusion = f32[512,384]{1,0:T(8,128)S(1)} fusion(f32[384,512]{1,0:T(8,128)S(1)} %fusion.2, f32[1,1,512,384]{3,2,1,0:T(8,128)S(1)} %copy-done.1, f32[384,384]{0,1:T(8,128)} %copy.7, s32[384]{0:T(512)S(1)} %iota_add_fusion, f32[384,384]{1,0:T(8,128)S(1)} %reduce_sum.9), kind=kOutput, calls=%fused_computation.1 | convolution fusion | flops 454066176 | bytes 3540480 | tf_op jit(solution)/shard_map/dot_general | solution.py:8
  161.7 1.8 %convolution_bitcast_fusion = f32[1,1,512,384]{3,2,1,0:T(8,128)} fusion(f32[512,384]{1,0:T(8,128)S(1)} %convolution_add_fusion, f32[384,384]{1,0:T(8,128)S(1)} %fusion.5), kind=kOutput, calls=%fused_computation | convolution fusion | flops 452984832 | bytes 2162688 | tf_op jit(solution)/shard_map/dot_general | solution.py:8
  (1 shorter events, 0.0 us)
Async XLA Ops:
  6.5 13.7 %copy-start = (f32[1,1,512,384]{3,2,1,0:T(8,128)S(1)}, f32[1,1,512,384]{3,2,1,0:T(8,128)}, u32[]{:S(2)}) copy-start(f32[1,1,512,384]{3,2,1,0:T(8,128)} %param.6) | copy-start | bytes 2359300
  6.5 152.6 %copy-start.1 = (f32[1,1,512,384]{3,2,1,0:T(8,128)S(1)}, f32[1,1,512,384]{3,2,1,0:T(8,128)}, u32[]{:S(2)}) copy-start(f32[1,1,512,384]{3,2,1,0:T(8,128)} %param.5) | copy-start | bytes 2359300
  6.5 142.4 %all-gather.4.cloned.1.call-start = ((), (), s32[]{:S(2)}) async-start(), calls=%async_computation | async-start | bytes 19464192 | tf_op jit(solution)/shard_map/all_gather | solution.py:30
Sparse Core Ops, SparseCore 0:
  23.9 124.9 all-gather.3
